TPU v7x, 32 devices: a whole 2x2x4 slice. The times are simulated.
32 devices in a mesh: expert: 8 (over z, x), tensor: 4 (over y, core).
Axes of the slice: x: 2, y: 2, z: 4, core: 2. Of those that a mesh axis runs over, the one named last changes fastest.
Arguments:
- tokens: bfloat16 [20480, 1024], P(('expert', 'tensor')), may hold values from -6 to 6
- cotangent: bfloat16 [20480, 1024], P(('expert', 'tensor')), may hold values from -6 to 6
- routes: int32 [20480, 1], P('expert'), may hold values from 0 to 7; in each aligned block of 640 rows (0 to 639, 640 to 1279, ...) at most 112 rows name the same one
- parents: int32 [8, 13], P('expert'), may hold values from 0 to 4, as said below
- ln_attn: float32 [1024], replicated, may hold values from 0.5 to 1.5
- w_qkv: bfloat16 [3, 1024, 1024], P(None, None, 'tensor'), may hold values from -0.1875 to 0.1875
- w_out: bfloat16 [1024, 1024], P('tensor'), may hold values from -3 to 3
- ln_mlp: float32 [1024], replicated, may hold values from 0.5 to 1.5
- w_up: bfloat16 [1024, 4096], P(None, 'tensor'), may hold values from -0.1875 to 0.1875
- w_down: bfloat16 [4096, 1024], P('tensor'), may hold values from -0.09375 to 0.09375
- w_router: bfloat16 [1024, 8], replicated, may hold values from -0.09375 to 0.09375
- w_mix: bfloat16 [1024, 2], replicated, may hold values from -0.1875 to 0.1875
- ex_up: bfloat16 [8, 1024, 4096], P('expert', None, 'tensor'), may hold values from -0.1875 to 0.1875
- ex_down: bfloat16 [8, 4096, 1024], P('expert', 'tensor')
Outputs:
- out: bfloat16 [20480, 1024], P(('expert', 'tensor'))
- grad_tokens: float32 [20480, 1024], P(('expert', 'tensor'))
- grad_ln_attn: float32 [1024], replicated
- grad_qkv: float32 [3, 1024, 1024], P(None, 'expert', 'tensor')
- grad_w_out: float32 [1024, 1024], P('tensor', 'expert')
- grad_ln_mlp: float32 [1024], P('expert')
- grad_up: float32 [1024, 4096], P('expert', 'tensor')
- grad_down: float32 [4096, 1024], P('tensor', 'expert')
- grad_router: float32 [1024, 8], P('expert')
- grad_mix: float32 [1024, 2], P('expert')
- grad_ex_up: float32 [8, 1024, 4096], P('expert', None, 'tensor')
- grad_ex_down: float32 [8, 4096, 1024], P('expert', 'tensor')
Inputs may be any that keep to these rules, and one draw needn't show every extreme that they name: `routes`: in each aligned block of 640 rows (the rows of one device), no expert is named by more than 112 rows, a bound that some block reaches. `parents`: entry j of a row is the parent segment of segment j. Entries 0 to 4 are 0 (the trunk and the four branches hang on the trunk); entries 5 to 12 (the leaves) name each branch 1 to 4 exactly twice.
All inputs are finite; a program needn't handle non-finite values.
Results may differ from a plain program's by a relative error of at most 0.017.
Values may be sent and summed in bfloat16 or wider, within the bound.
No kernel may reach another device: no remote copies, remote signals or barrier semaphores. Data moves between devices by JAX's collectives and lax.ppermute only.
A program may use at most 320 MiB of HBM per device.

v0:
```python
import jax
import jax.numpy as jnp
from jax import lax
from jax.sharding import PartitionSpec as P

HEAD_DIM = 64
TRUNK = 1024
SEG = 128
SEGS = 13
QBLK = 512
TREE_LEN = 2560
EPSILON = 1e-05
NEGATIVE_FILL = -1e30


def norm_parts(values):
    row_mean = jnp.mean(values, axis=-1, keepdims=True)
    centred = values - row_mean
    row_var = jnp.mean(centred * centred, axis=-1, keepdims=True)
    inverse = lax.rsqrt(row_var + EPSILON)
    return (centred * inverse, inverse)


def norm_back(grad_normed, gain_vec, scaled, inverse):
    grad_scaled = grad_normed * gain_vec
    first_mean = jnp.mean(grad_scaled, axis=-1, keepdims=True)
    second = jnp.mean(grad_scaled * scaled, axis=-1, keepdims=True)
    return inverse * (grad_scaled - first_mean - scaled * second)


def gelu_exact(values):
    return jax.nn.gelu(values, approximate=False)


def gelu_slope(values):
    return (
        0.5 * (1.0 + lax.erf(values * 0.7071067811865476))
        + values * jnp.exp(-0.5 * values * values) * 0.3989422804014327
    )


def segment_of(position):
    return jnp.where(position < TRUNK, 0, 1 + (position - TRUNK) // SEG)


def path_mask(parents_row, query_pos, key_pos):
    seg_ids = jnp.arange(SEGS, dtype=jnp.int32)
    query_seg = segment_of(query_pos)
    key_seg = segment_of(key_pos)
    parent_seg = jnp.sum(
        jnp.where(query_seg[:, None] == seg_ids[None, :], parents_row[None, :], 0), axis=1
    )
    grand_seg = jnp.sum(
        jnp.where(parent_seg[:, None] == seg_ids[None, :], parents_row[None, :], 0), axis=1
    )
    on_path = (
        (key_seg[None, :] == query_seg[:, None])
        | (key_seg[None, :] == parent_seg[:, None])
        | (key_seg[None, :] == grand_seg[:, None])
    )
    return on_path & (key_pos[None, :] <= query_pos[:, None])


def block_inputs(qkv_rows, parents, block_index):
    row_start = block_index * QBLK
    tree_index = row_start // TREE_LEN
    queries = lax.dynamic_slice_in_dim(qkv_rows[0], row_start, QBLK, 0).reshape(QBLK, -1, HEAD_DIM)
    key_rows = qkv_rows[1].reshape(TREE_LEN, -1, HEAD_DIM)
    values = qkv_rows[2].reshape(TREE_LEN, -1, HEAD_DIM)
    parents_row = lax.dynamic_index_in_dim(parents, tree_index, 0, keepdims=False)
    raw_scores = jnp.einsum(
        "qhd,khd->hqk", queries, key_rows, preferred_element_type=jnp.float32
    ) * HEAD_DIM ** (-0.5)
    first_row = row_start - tree_index * TREE_LEN
    allowed = path_mask(
        parents_row,
        first_row + jnp.arange(QBLK, dtype=jnp.int32),
        jnp.arange(TREE_LEN, dtype=jnp.int32),
    )
    scores = jnp.where(allowed[None], raw_scores, NEGATIVE_FILL)
    return (row_start, tree_index, queries, key_rows, values, scores)


def to_owners(values, expert_ids, quarter, slot_index, experts, quarters, capacity):
    width = values.shape[1]
    outgoing = jnp.zeros((experts, quarters, capacity, width), jnp.bfloat16)
    outgoing = outgoing.at[expert_ids, quarter, slot_index].set(values)
    return lax.all_to_all(outgoing, "expert", split_axis=0, concat_axis=0, tiled=True)


def to_sources(parts):
    return lax.all_to_all(
        parts.astype(jnp.bfloat16), "expert", split_axis=0, concat_axis=0, tiled=True
    ).astype(parts.dtype)


def per_device(
    tokens,
    cotangent,
    routes,
    parents,
    ln_attn,
    w_qkv,
    w_out,
    ln_mlp,
    w_up,
    w_down,
    w_router,
    w_mix,
    ex_up,
    ex_down,
):
    tok_dev = tokens.shape[0]
    model_width = tokens.shape[1]
    quarters = lax.axis_size("tensor")
    own_start = lax.axis_index("tensor") * tok_dev
    group_rows = tok_dev * quarters
    experts = w_router.shape[1]
    capacity = max(2, tok_dev * 7 // (5 * experts))
    block_total = group_rows // QBLK
    gathered = lax.all_gather(tokens, "tensor", axis=0, tiled=True)
    scaled_one, inverse_one = norm_parts(gathered.astype(jnp.float32))
    normed_one = (scaled_one * ln_attn).astype(jnp.bfloat16)
    qkv_rows = jnp.einsum(
        "td,sdc->stc", normed_one, w_qkv, preferred_element_type=jnp.float32
    ).astype(jnp.bfloat16)

    def attend_block(block_index):
        row_start, tree_index, queries, key_rows, values, scores = block_inputs(
            qkv_rows, parents, block_index
        )
        row_max = jnp.max(scores, axis=-1, keepdims=True)
        weights = jnp.exp(scores - row_max)
        row_total = jnp.sum(weights, axis=-1, keepdims=True)
        weights = (weights / row_total).astype(jnp.bfloat16)
        output = jnp.einsum("hqk,khd->qhd", weights, values, preferred_element_type=jnp.float32)
        return (
            output.reshape(QBLK, -1).astype(jnp.bfloat16),
            (row_max + jnp.log(row_total))[..., 0],
        )

    attended, log_total = lax.map(attend_block, jnp.arange(block_total, dtype=jnp.int32))
    attended = attended.reshape(group_rows, -1)
    residual = tokens.astype(jnp.float32) + lax.psum_scatter(
        jnp.dot(attended, w_out, preferred_element_type=jnp.float32),
        "tensor",
        scatter_dimension=0,
        tiled=True,
    )
    residual_all = lax.all_gather(residual, "tensor", axis=0, tiled=True)
    scaled_two, inverse_two = norm_parts(residual_all)
    normed_two = (scaled_two * ln_mlp).astype(jnp.bfloat16)
    pre_dense = jnp.dot(normed_two, w_up, preferred_element_type=jnp.float32)
    active = gelu_exact(pre_dense).astype(jnp.bfloat16)
    dense_part = jnp.dot(active, w_down, preferred_element_type=jnp.float32)
    router_probs = jax.nn.softmax(
        jnp.dot(normed_two, w_router, preferred_element_type=jnp.float32), axis=-1
    )
    expert_ids = routes[:, 0]
    chosen = expert_ids[:, None] == jnp.arange(experts, dtype=jnp.int32)[None, :]
    gate_prob = jnp.sum(jnp.where(chosen, router_probs, 0.0), axis=1)
    mix_coef = jax.nn.softmax(
        jnp.dot(normed_two, w_mix, preferred_element_type=jnp.float32), axis=-1
    )
    counted = chosen.astype(jnp.int32).reshape(quarters, tok_dev, experts)
    position = (jnp.cumsum(counted, axis=1) - 1).reshape(group_rows, experts)
    slot_index = jnp.sum(jnp.where(chosen, position, 0), axis=1)
    quarter = jnp.arange(group_rows, dtype=jnp.int32) // tok_dev
    arrived = to_owners(normed_two, expert_ids, quarter, slot_index, experts, quarters, capacity)
    flat_rows = arrived.reshape(-1, model_width)
    expert_pre = jnp.dot(flat_rows, ex_up[0], preferred_element_type=jnp.float32)
    expert_active = gelu_exact(expert_pre).astype(jnp.bfloat16)
    expert_part = jnp.dot(expert_active, ex_down[0], preferred_element_type=jnp.float32).reshape(
        arrived.shape
    )
    returned = to_sources(expert_part)
    expert_weight = mix_coef[:, 1] * gate_prob
    expert_rows = returned[expert_ids, quarter, slot_index]
    extra_term = 0.0
    dense_coef = mix_coef[:, 0]
    mixed = (
        lax.psum_scatter(
            (dense_coef[:, None] * dense_part + expert_weight[:, None] * expert_rows).astype(
                jnp.bfloat16
            ),
            "tensor",
            scatter_dimension=0,
            tiled=True,
        ).astype(jnp.float32)
        + extra_term
    )
    out = (residual + mixed).astype(jnp.bfloat16)
    grad_all = lax.all_gather(cotangent, "tensor", axis=0, tiled=True).astype(jnp.float32)
    grad_dense = (mix_coef[:, 0:1] * grad_all).astype(jnp.bfloat16)
    grad_down = jnp.einsum("gf,gd->fd", active, grad_dense, preferred_element_type=jnp.float32)
    grad_active = jnp.einsum("gd,fd->gf", grad_dense, w_down, preferred_element_type=jnp.float32)
    grad_pre = (grad_active * gelu_slope(pre_dense)).astype(jnp.bfloat16)
    grad_up = jnp.einsum("gd,gf->df", normed_two, grad_pre, preferred_element_type=jnp.float32)
    grad_normed_two = jnp.einsum("gf,df->gd", grad_pre, w_up, preferred_element_type=jnp.float32)
    dense_dot = jnp.sum(grad_all * dense_part, axis=1)
    grad_expert = (expert_weight[:, None] * grad_all).astype(jnp.bfloat16)
    arrived_grad = to_owners(
        grad_expert, expert_ids, quarter, slot_index, experts, quarters, capacity
    )
    flat_grad = arrived_grad.reshape(-1, model_width)
    grad_ex_down = jnp.einsum(
        "rf,rd->fd", expert_active, flat_grad, preferred_element_type=jnp.float32
    )[None]
    grad_ex_active = jnp.einsum(
        "rd,fd->rf", flat_grad, ex_down[0], preferred_element_type=jnp.float32
    )
    grad_ex_pre = (grad_ex_active * gelu_slope(expert_pre)).astype(jnp.bfloat16)
    grad_ex_up = jnp.einsum(
        "rd,rf->df", flat_rows, grad_ex_pre, preferred_element_type=jnp.float32
    )[None]
    grad_ex_rows = jnp.einsum(
        "rf,df->rd", grad_ex_pre, ex_up[0], preferred_element_type=jnp.float32
    ).reshape(arrived.shape)
    grad_back = to_sources(grad_ex_rows)
    grad_normed_two = grad_normed_two + grad_back[expert_ids, quarter, slot_index]
    expert_dot = jnp.sum(grad_all * expert_rows, axis=1)
    row_dots = jnp.stack([dense_dot, expert_dot], axis=1)
    grad_normed_two, row_dots = (
        lax.psum(grad_normed_two.astype(jnp.bfloat16), "tensor").astype(jnp.float32),
        lax.psum(row_dots.astype(jnp.bfloat16), "tensor").astype(jnp.float32),
    )
    mix_grad = jnp.stack([row_dots[:, 0], gate_prob * row_dots[:, 1]], axis=1)
    grad_mix_logits = (
        mix_coef * (mix_grad - jnp.sum(mix_coef * mix_grad, axis=1, keepdims=True))
    ).astype(jnp.bfloat16)
    grad_gate = mix_coef[:, 1] * row_dots[:, 1]
    grad_router_logits = (
        router_probs
        * (jnp.where(chosen, grad_gate[:, None], 0.0) - (gate_prob * grad_gate)[:, None])
    ).astype(jnp.bfloat16)
    grad_normed_two = grad_normed_two + jnp.einsum(
        "ge,de->gd", grad_router_logits, w_router, preferred_element_type=jnp.float32
    )
    grad_normed_two = grad_normed_two + jnp.einsum(
        "gm,dm->gd", grad_mix_logits, w_mix, preferred_element_type=jnp.float32
    )
    grad_router = jnp.einsum(
        "gd,ge->de", normed_two, grad_router_logits, preferred_element_type=jnp.float32
    )
    grad_mix = jnp.einsum(
        "gd,gm->dm", normed_two, grad_mix_logits, preferred_element_type=jnp.float32
    )
    grad_ln_mlp = jnp.sum(grad_normed_two * scaled_two, axis=0)
    grad_residual = grad_all + norm_back(grad_normed_two, ln_mlp, scaled_two, inverse_two)
    grad_branch = grad_residual.astype(jnp.bfloat16)
    grad_w_out = jnp.einsum("gc,gd->cd", attended, grad_branch, preferred_element_type=jnp.float32)
    grad_attended = jnp.einsum(
        "gd,cd->gc", grad_branch, w_out, preferred_element_type=jnp.float32
    ).astype(jnp.bfloat16)

    def attend_back(carried, block_index):
        grad_keys, grad_values = carried
        row_start, tree_index, queries, key_rows, values, scores = block_inputs(
            qkv_rows, parents, block_index
        )
        log_block = lax.dynamic_index_in_dim(log_total, block_index, 0, keepdims=False)
        weights = jnp.exp(scores - log_block[..., None])
        grad_block = lax.dynamic_slice_in_dim(grad_attended, row_start, QBLK, 0).reshape(
            QBLK, -1, HEAD_DIM
        )
        grad_weights = jnp.einsum(
            "qhd,khd->hqk", grad_block, values, preferred_element_type=jnp.float32
        )
        inner = jnp.sum(weights * grad_weights, axis=-1, keepdims=True)
        grad_scores = (weights * (grad_weights - inner)).astype(jnp.bfloat16)
        grad_query = jnp.einsum(
            "hqk,khd->qhd", grad_scores, key_rows, preferred_element_type=jnp.float32
        ) * HEAD_DIM ** (-0.5)
        key_part = jnp.einsum(
            "hqk,qhd->khd", grad_scores, queries, preferred_element_type=jnp.float32
        ) * HEAD_DIM ** (-0.5)
        value_part = jnp.einsum(
            "hqk,qhd->khd",
            weights.astype(jnp.bfloat16),
            grad_block,
            preferred_element_type=jnp.float32,
        )
        grad_keys = grad_keys + key_part.reshape(TREE_LEN, -1)
        grad_values = grad_values + value_part.reshape(TREE_LEN, -1)
        return ((grad_keys, grad_values), grad_query.reshape(QBLK, -1).astype(jnp.bfloat16))

    empty_rows = jnp.zeros((group_rows, qkv_rows.shape[2]), jnp.float32)
    (grad_keys, grad_values), grad_queries = lax.scan(
        attend_back, (empty_rows, empty_rows), jnp.arange(block_total, dtype=jnp.int32)
    )
    grad_qkv_rows = jnp.stack(
        [
            grad_queries.reshape(group_rows, -1),
            grad_keys.astype(jnp.bfloat16),
            grad_values.astype(jnp.bfloat16),
        ]
    )
    grad_w_qkv = jnp.einsum(
        "gd,sgc->sdc", normed_one, grad_qkv_rows, preferred_element_type=jnp.float32
    )
    grad_normed_one = jnp.einsum(
        "sgc,sdc->gd", grad_qkv_rows, w_qkv, preferred_element_type=jnp.float32
    )
    part_gain = jnp.sum(grad_normed_one * scaled_one, axis=0)
    grad_normed_own = lax.psum_scatter(
        grad_normed_one.astype(jnp.bfloat16), "tensor", scatter_dimension=0, tiled=True
    ).astype(jnp.float32)
    own_scaled = lax.dynamic_slice_in_dim(scaled_one, own_start, tok_dev, 0)
    own_inverse = lax.dynamic_slice_in_dim(inverse_one, own_start, tok_dev, 0)
    own_residual_grad = lax.dynamic_slice_in_dim(grad_residual, own_start, tok_dev, 0)
    grad_tokens = own_residual_grad + norm_back(grad_normed_own, ln_attn, own_scaled, own_inverse)
    summed_grads = (
        lax.psum_scatter(grad_w_qkv, "expert", scatter_dimension=1, tiled=True),
        lax.psum_scatter(grad_w_out, "expert", scatter_dimension=1, tiled=True),
        lax.psum_scatter(grad_ln_mlp, "expert", scatter_dimension=0, tiled=True),
        lax.psum_scatter(grad_up, "expert", scatter_dimension=0, tiled=True),
        lax.psum_scatter(grad_down, "expert", scatter_dimension=1, tiled=True),
        lax.psum_scatter(grad_router, "expert", scatter_dimension=0, tiled=True),
        lax.psum_scatter(grad_mix, "expert", scatter_dimension=0, tiled=True),
    )
    grad_ln_attn = lax.psum(part_gain, ("expert", "tensor"))
    return (
        out,
        grad_tokens,
        grad_ln_attn,
        summed_grads[0],
        summed_grads[1],
        summed_grads[2],
        summed_grads[3],
        summed_grads[4],
        summed_grads[5],
        summed_grads[6],
        grad_ex_up,
        grad_ex_down,
    )


def solution(mesh):
    return jax.shard_map(
        per_device,
        mesh=mesh,
        in_specs=(
            P(("expert", "tensor"), None),
            P(("expert", "tensor"), None),
            P("expert", None),
            P("expert", None),
            P(),
            P(None, None, "tensor"),
            P("tensor", None),
            P(),
            P(None, "tensor"),
            P("tensor", None),
            P(),
            P(),
            P("expert", None, "tensor"),
            P("expert", "tensor", None),
        ),
        out_specs=(
            P(("expert", "tensor"), None),
            P(("expert", "tensor"), None),
            P(),
            P(None, "expert", "tensor"),
            P("tensor", "expert"),
            P("expert"),
            P("expert", "tensor"),
            P("tensor", "expert"),
            P("expert", None),
            P("expert", None),
            P("expert", None, "tensor"),
            P("expert", "tensor", None),
        ),
        check_vma=False,
    )
```

profile of v0, /device:TPU:0, one launch (start us, length us, event | category | flops | bytes accessed | tf_op | source)
XLA Modules:
  0.0 2363.1 jit_solution(15836324658128825775)
XLA Ops:
  8.0 44.8 %all-gather.4.cloned.1.call-done = bf16[2560,1024]{1,0:T(8,128)(2,1)} async-done(((bf16[640,1024]{1,0:T(8,128)(2,1)}), bf16[2560,1024]{1,0:T(8,128)(2,1)}) %all-gather.4.cloned.1.call-update) | async-done | bytes 5242896 | tf_op jit(solution)/shard_map/all_gather | solution.py:121
  75.0 190.0 %while.33 = (s32[]{:T(128)}, bf16[5,512,256]{2,1,0:T(8,128)(2,1)}, f32[5,4,512]{2,1,0:T(4,128)S(1)}, s32[5]{0:T(128)S(1)}, s32[1,13]{1,0:T(1,128)S(1)}, /*index=...) while((s32[]{:T(128)}, bf16[5,512,256]{2,1,0:T(8,128)(2,1)}, ...), condition=%wide.region_7.8_spmd, body=%wide.region_2.7_spmd.sunk | while | flops 1414493696 | bytes 169976272 | solution.py:142
  272.6 85.0 %reduce-scatter.12.cloned.1.call-done = f32[640,1024]{1,0:T(8,128)} async-done(((f32[2560,1024]{1,0:T(8,128)}), f32[640,1024]{1,0:T(8,128)}) %reduce-scatter.12.cloned.1.call-update) | async-done | bytes 2621456 | tf_op jit(solution)/shard_map/reduce_scatter | solution.py:144
  368.6 63.2 %all-gather.6.cloned.1.call-done = f32[2560,1024]{1,0:T(8,128)} async-done(((f32[640,1024]{1,0:T(8,128)}), f32[2560,1024]{1,0:T(8,128)}) %all-gather.6.cloned.1.call-update) | async-done | bytes 10485776 | tf_op jit(solution)/shard_map/all_gather | solution.py:150
  441.6 18.1 scatter_custom_fusion
  459.7 166.5 %all_to_all.20 = bf16[8,4,112,1024]{3,2,1,0:T(8,128)(2,1)S(1)} all-to-all(bf16[8,4,112,1024]{3,2,1,0:T(8,128)(2,1)} %bitcast.211), channel_id=1, replica_groups=mesh['expert'=8,'tensor'=4] {'expert'}, dimensions={0} | all-to-all | bytes 14680064 | tf_op jit(solution)/shard_map/all_to_all | solution.py:88
  626.2 40.2 %fusion.43 = (bf16[3584,1024]{1,0:T(8,128)(2,1)S(1)}, f32[3584,1024]{1,0:T(8,128)}) fusion(bf16[3584,1024]{1,0:T(8,128)(2,1)S(1)} %bitcast.215, bf16[1,1024,1024]{2,1,0:T(8,128)(2,1)S(1)} %copy-done), kind=kOutput, calls=%fused_computation.106 | convolution fusion | flops 7754743808 | bytes 31457280 | tf_op jit(solution)/shard_map/dot_general | solution.py:171
  694.0 29.9 %fusion.62 = (bf16[2560,1024]{1,0:T(8,128)(2,1)}, f32[2560,1024]{1,0:T(8,128)}) fusion(bf16[2560,1024]{1,0:T(8,128)(2,1)S(1)} %multiply_convert_fusion.1, bf16[1024,1024]{1,0:T(8,128)(2,1)S(1)} %copy-done.58), kind=kOutput, calls=%fused_computation.135 | convolution fusion | flops 5539102720 | bytes 23068672 | tf_op jit(solution)/shard_map/dot_general | solution.py:153
  723.9 120.1 %all-to-all-done.1 = bf16[8,4,112,1024]{3,2,1,0:T(8,128)(2,1)} async-done(((bf16[8,4,112,1024]{3,2,1,0:T(8,128)(2,1)}), bf16[8,4,112,1024]{3,2,1,0:T(8,128)(2,1)}, u32[]{:S(2)}, u32[]{:S(2)}) %all-to-all-start.1) | async-done | bytes 7340064 | tf_op jit(solution)/shard_map/all_to_all | solution.py:92
  854.2 40.0 %gather_fusion = f32[2560,1024]{1,0:T(8,128)} fusion(f32[8,4,112,1024]{3,2,1,0:T(8,128)} %convert_element_type.171, s32[2560]{0:T(1024)S(1)} %copy-done.3), kind=kCustom, calls=%fused_computation | custom fusion | bytes 21002240 | tf_op jit(solution)/shard_map/gather | solution.py:178
  894.2 15.1 fusion.71
  919.9 17.8 scatter_custom_fusion.1
  937.7 164.2 %all_to_all.21 = bf16[8,4,112,1024]{3,2,1,0:T(8,128)(2,1)S(1)} all-to-all(bf16[8,4,112,1024]{3,2,1,0:T(8,128)(2,1)} %bitcast.212), channel_id=1, replica_groups=mesh['expert'=8,'tensor'=4] {'expert'}, dimensions={0} | all-to-all | bytes 14680064 | tf_op jit(solution)/shard_map/all_to_all | solution.py:88
  1101.9 15.5 fusion.49
  1148.6 146.3 %all-to-all-done.3 = bf16[8,4,112,1024]{3,2,1,0:T(8,128)(2,1)} async-done(((bf16[8,4,112,1024]{3,2,1,0:T(8,128)(2,1)}), bf16[8,4,112,1024]{3,2,1,0:T(8,128)(2,1)}, u32[]{:S(2)}, u32[]{:S(2)}) %all-to-all-start.3) | async-done | bytes 7340064 | tf_op jit(solution)/shard_map/all_to_all | solution.py:92
  1305.1 40.0 %gather_fusion.1 = f32[2560,1024]{1,0:T(8,128)} fusion(f32[8,4,112,1024]{3,2,1,0:T(8,128)} %convert_element_type.181, s32[2560]{0:T(1024)S(1)} %copy-done.3), kind=kCustom, calls=%fused_computation.1 | custom fusion | bytes 21002240 | tf_op jit(solution)/shard_map/gather | solution.py:220
  1378.1 79.8 %all-reduce.3.cloned.1.call-done = bf16[2560,1024]{1,0:T(8,128)(2,1)} async-done(((bf16[2560,1024]{1,0:T(8,128)(2,1)}), bf16[2560,1024]{1,0:T(8,128)(2,1)}) %all-reduce.3.cloned.1.call-update) | async-done | bytes 5242896 | tf_op jit(solution)/shard_map/psum | solution.py:224
  1482.8 420.8 %while.34 = (s32[]{:T(128)}, f32[2560,256]{0,1:T(8,128)}, f32[2560,256]{0,1:T(8,128)}, bf16[5,512,256]{2,1,0:T(8,128)(2,1)}, bf16[3,2560,256]{1,2,0:T(8,128)(2,1...) while((s32[]{:T(128)}, f32[2560,256]{0,1:T(8,128)}, ...), condition=%wide.region_33.34_spmd.clone, body=%wide.region_29.33_spmd.clone.sunk | while | flops 3446896640 | bytes 251757168 | solution.py:288
  1513.3 15.1 multiply_reduce_fusion.11
  1528.3 22.2 multiply_convert_fusion.9
  1614.1 20.0 multiply_convert_fusion.9
  1682.6 15.1 multiply_reduce_fusion.11
  1697.7 20.0 multiply_convert_fusion.9
  1766.2 15.1 multiply_reduce_fusion.11
  1781.2 20.0 multiply_convert_fusion.9
  1864.8 20.0 multiply_convert_fusion.9
  1992.2 21.0 all-reduce
  2025.4 37.2 %psum.23 = f32[1024]{0:T(1024)} all-reduce(f32[1024]{0:T(1024)S(1)} %get-tuple-element.473), channel_id=1, replica_groups=mesh['expert'=8,'tensor'=4] {'expert','tensor'}, use_global_device_ids=true, to_apply=%region_38.39 | all-reduce | flops 1024 | bytes 8192 | tf_op jit(solution)/shard_map/psum | solution.py:321
  2072.4 32.0 %reduce-scatter.26.cloned.1.call-done = f32[128,8]{0,1:T(8,128)} async-done(((f32[1024,8]{0,1:T(8,128)}), f32[128,8]{0,1:T(8,128)}) %reduce-scatter.26.cloned.1.call-update) | async-done | bytes 4112 | tf_op jit(solution)/shard_map/reduce_scatter | solution.py:318
  2104.4 92.0 %reduce-scatter.24.cloned.1.call-done = f32[1024,128]{1,0:T(8,128)} async-done(((f32[1024,1024]{1,0:T(8,128)}), f32[1024,128]{1,0:T(8,128)}) %reduce-scatter.24.cloned.1.call-update) | async-done | bytes 524304 | tf_op jit(solution)/shard_map/reduce_scatter | solution.py:317
  2196.4 91.9 %reduce-scatter.22.cloned.1.call-done = f32[128,1024]{1,0:T(8,128)} async-done(((f32[1024,1024]{1,0:T(8,128)}), f32[128,1024]{1,0:T(8,128)}) %reduce-scatter.22.cloned.1.call-update) | async-done | bytes 524304 | tf_op jit(solution)/shard_map/reduce_scatter | solution.py:316
  2288.3 68.0 %reduce-scatter.20.cloned.1.call-done = f32[256,128]{1,0:T(8,128)} async-done(((f32[256,1024]{1,0:T(8,128)}), f32[256,128]{1,0:T(8,128)}) %reduce-scatter.20.cloned.1.call-update) | async-done | bytes 131088 | tf_op jit(solution)/shard_map/reduce_scatter | solution.py:314
  (477 shorter events, 753.4 us)
Async XLA Ops:
  7.2 619.0 %copy-start = (bf16[1,1024,1024]{2,1,0:T(8,128)(2,1)S(1)}, bf16[1,1024,1024]{2,1,0:T(8,128)(2,1)}, u32[]{:S(2)}) copy-start(bf16[1,1024,1024]{2,1,0:T(8,128)(2,1)} %param.30) | copy-start | bytes 6291460
  7.2 45.6 %all-gather.4.cloned.1.call-start = ((), (), s32[]{:S(2)}) async-start(), calls=%async_computation.13 | async-start | bytes 6553600 | tf_op jit(solution)/shard_map/all_gather | solution.py:121
  7.9 349.6 %reduce-scatter.12.cloned.1.call-start = ((), (), s32[]{:S(2)}) async-start(), calls=%async_computation.14 | async-start | bytes 13107200 | tf_op jit(solution)/shard_map/reduce_scatter | solution.py:144
  265.0 92.6 %copy-start.16 = (bf16[640,1024]{1,0:T(8,128)(2,1)S(1)}, bf16[640,1024]{1,0:T(8,128)(2,1)}, u32[]{:S(2)}) copy-start(bf16[640,1024]{1,0:T(8,128)(2,1)} %param.18) | copy-start | bytes 3932164
  272.1 89.4 %copy-start.45 = (s32[2560,1]{0,1:T(1,128)S(1)}, s32[2560,1]{0,1:T(1,128)}, u32[]{:S(2)}) copy-start(s32[2560,1]{0,1:T(1,128)} %param.20) | copy-start | bytes 30724
  272.1 96.3 %copy-start.54 = (s32[3]{0:T(128)S(1)}, s32[3]{0:T(128)}, u32[]{:S(2)}) copy-start(s32[3]{0:T(128)} %constant.392) | copy-start | bytes 40
  272.1 96.4 %copy-start.53 = (s32[3]{0:T(128)S(1)}, s32[3]{0:T(128)}, u32[]{:S(2)}) copy-start(s32[3]{0:T(128)} %constant.395) | copy-start | bytes 40
  272.1 159.7 %all-gather.6.cloned.1.call-start = ((), (), s32[]{:S(2)}) async-start(), calls=%async_computation.15 | async-start | bytes 13107200 | tf_op jit(solution)/shard_map/all_gather | solution.py:150
  361.5 331.9 %copy-start.27 = (s32[2560]{0:T(1024)}, s32[2560]{0:T(1024)S(1)}, u32[]{:S(2)}) copy-start(s32[2560]{0:T(1024)S(1)} %reduce.8) | copy-start | bytes 30724
  436.3 248.5 %copy-start.23 = (f32[2560]{0:T(1024)}, f32[2560]{0:T(1024)S(1)}, u32[]{:S(2)}) copy-start(f32[2560]{0:T(1024)S(1)} %broadcast_multiply_fusion.2) | copy-start | bytes 30724
  441.6 243.2 %copy-start.25 = (f32[2560]{0:T(1024)}, f32[2560]{0:T(1024)S(1)}, u32[]{:S(2)}) copy-start(f32[2560]{0:T(1024)S(1)} %add_rsqrt_fusion) | copy-start | bytes 30724
  679.3 164.8 %all-to-all-start.1 = ((bf16[8,4,112,1024]{3,2,1,0:T(8,128)(2,1)}), bf16[8,4,112,1024]{3,2,1,0:T(8,128)(2,1)}, u32[]{:S(2)}, u32[]{:S(2)}) async-start(bf16[8,4,112,1024]{3,2,1,0:T(8,128)(2,1)} %convolution_convert_fusion.1), calls=%async_computation.2 | async-start | bytes 14680064 | tf_op jit(solution)/shard_map/all_to_all | solution.py:92
  684.2 210.0 %all-gather.8.cloned.1.call-start = ((), (), s32[]{:S(2)}) async-start(), calls=%async_computation.17 | async-start | bytes 6553600 | tf_op jit(solution)/shard_map/all_gather | solution.py:193
  723.9 130.3 %copy-start.3 = (s32[2560]{0:T(1024)S(1)}, s32[2560]{0:T(1024)}, u32[]{:S(2)}) copy-start(s32[2560]{0:T(1024)} %get-tuple-element.475) | copy-start | bytes 30724
  919.9 441.7 %copy-start.43 = (f32[2560]{0:T(1024)}, f32[2560]{0:T(1024)S(1)}, u32[]{:S(2)}) copy-start(f32[2560]{0:T(1024)S(1)} %get-tuple-element.426) | copy-start | bytes 30724
  937.7 164.2 %copy-start.56 = (bf16[1,1024,1024]{2,1,0:T(8,128)(2,1)S(1)}, bf16[1,1024,1024]{2,1,0:T(8,128)(2,1)}, u32[]{:S(2)}) copy-start(bf16[1,1024,1024]{2,1,0:T(8,128)(2,1)} %param.31) | copy-start | bytes 6291460
  1130.4 164.5 %all-to-all-start.3 = ((bf16[8,4,112,1024]{3,2,1,0:T(8,128)(2,1)}), bf16[8,4,112,1024]{3,2,1,0:T(8,128)(2,1)}, u32[]{:S(2)}, u32[]{:S(2)}) async-start(bf16[8,4,112,1024]{3,2,1,0:T(8,128)(2,1)} %convolution_convert_fusion), calls=%async_computation.5 | async-start | bytes 14680064 | tf_op jit(solution)/shard_map/all_to_all | solution.py:92
  1135.5 322.4 %all-reduce.3.cloned.1.call-start = ((), (), s32[]{:S(2)}) async-start(), calls=%async_computation.18 | async-start | bytes 10485760 | tf_op jit(solution)/shard_map/psum | solution.py:224
  1356.6 600.3 %reduce-scatter.28.cloned.1.call-start = ((), (), s32[]{:S(2)}) async-start(), calls=%async_computation.25 | async-start | bytes 589824
  1372.1 85.8 %copy-start.24 = (f32[2560]{0:T(1024)S(1)}, f32[2560]{0:T(1024)}, u32[]{:S(2)}) copy-start(f32[2560]{0:T(1024)} %copy-done.23) | copy-start | bytes 30724
  1372.1 85.8 %copy-start.26 = (f32[2560]{0:T(1024)S(1)}, f32[2560]{0:T(1024)}, u32[]{:S(2)}) copy-start(f32[2560]{0:T(1024)} %copy-done.25) | copy-start | bytes 30724
  1372.1 586.2 %reduce-scatter.14.cloned.1.call-start = ((), (), s32[]{:S(2)}) async-start(), calls=%async_computation.16 | async-start | bytes 6553600 | tf_op jit(solution)/shard_map/reduce_scatter | solution.py:182
  1378.0 684.6 %reduce-scatter.18.cloned.1.call-start = ((), (), s32[]{:S(2)}) async-start(), calls=%async_computation.20 | async-start | bytes 3538944 | tf_op jit(solution)/shard_map/reduce_scatter | solution.py:313
  1482.8 425.6 %copy-start.34 = (f32[2560]{0:T(1024)S(1)}, f32[2560]{0:T(1024)}, u32[]{:S(2)}) copy-start(f32[2560]{0:T(1024)} %copy-done.33) | copy-start | bytes 30724
  1482.8 425.6 %copy-start.38 = (f32[2560]{0:T(1024)S(1)}, f32[2560]{0:T(1024)}, u32[]{:S(2)}) copy-start(f32[2560]{0:T(1024)} %copy-done.37) | copy-start | bytes 30724
  1482.8 425.6 %copy-start.50 = (f32[1024]{0:T(1024)S(1)}, f32[1024]{0:T(1024)}, u32[]{:S(2)}) copy-start(f32[1024]{0:T(1024)} %param.22) | copy-start | bytes 12292
  1918.2 146.4 %reduce-scatter.16.cloned.1.call-start = ((), (), s32[]{:S(2)}) async-start(), calls=%async_computation.19 | async-start | bytes 6553600 | tf_op jit(solution)/shard_map/reduce_scatter | solution.py:305
  1930.1 174.3 %reduce-scatter.26.cloned.1.call-start = ((), (), s32[]{:S(2)}) async-start(), calls=%async_computation.24 | async-start | bytes 36864 | tf_op jit(solution)/shard_map/reduce_scatter | solution.py:318
  1934.1 262.3 %reduce-scatter.24.cloned.1.call-start = ((), (), s32[]{:S(2)}) async-start(), calls=%async_computation.23 | async-start | bytes 4718592 | tf_op jit(solution)/shard_map/reduce_scatter | solution.py:317
  1944.9 343.4 %reduce-scatter.22.cloned.1.call-start = ((), (), s32[]{:S(2)}) async-start(), calls=%async_computation.22 | async-start | bytes 4718592 | tf_op jit(solution)/shard_map/reduce_scatter | solution.py:316
  1955.5 400.8 %reduce-scatter.20.cloned.1.call-start = ((), (), s32[]{:S(2)}) async-start(), calls=%async_computation.21 | async-start | bytes 1179648 | tf_op jit(solution)/shard_map/reduce_scatter | solution.py:314
  2013.8 342.5 %copy-start.1 = (bf16[1,1024,1024]{2,1,0:T(8,128)(2,1)S(1)}, bf16[1,1024,1024]{2,1,0:T(8,128)(2,1)}, u32[]{:S(2)}) copy-start(bf16[1,1024,1024]{2,1,0:T(8,128)(2,1)} %param.30) | copy-start | bytes 6291460
  (78 other events, 1057.1 us)
Sparse Core Ops, SparseCore 0:
  9.6 43.1 all-gather.3
  272.2 85.2 reduce-scatter.11
  361.6 70.1 all-gather.5
  686.3 40.8 all-gather.7
  1356.7 101.0 all-reduce.2
  1461.1 62.0 reduce-scatter.27
  1525.9 50.3 reduce-scatter.13
  1918.3 74.8 reduce-scatter.17
  1995.7 51.2 reduce-scatter.15
  2050.8 53.5 reduce-scatter.25
  2109.0 87.2 reduce-scatter.23
  2200.4 87.8 reduce-scatter.21
  2292.6 63.6 reduce-scatter.19
where the time goes:
time: 2370 us; the launch traced here: 2360 us
  waiting for transfers between devices  825 us (35%)
  matrix products  585 us (25%)
  blocking collectives  399 us (17%)
  other arithmetic  293 us (12%)
  local copies, waits for them, and re-layouts  217 us (9%)
    all_to_all x2, blocking collectives, to_owners(): lax.all_to_all(outgoing, 'expert', split_axis=0, concat_axis=0, tiled=True)  331 us
    all_to_all x2, waiting for transfers between devices, to_sources(): lax.all_to_all(parts.astype(jnp.bfloat16), 'expert', split_axis=0, concat...  266 us
    convert_element_type x5, other arithmetic, attend_back(): grad_scores = (weights * (grad_weights - inner)).astype(jnp.bfloat16)  102 us
    reduce_scatter x1, waiting for transfers between devices, per_device(): lax.psum_scatter(grad_down, 'expert', scatter_dimension=1, tiled=True)  92 us
    reduce_scatter x1, waiting for transfers between devices, per_device(): lax.psum_scatter(grad_up, 'expert', scatter_dimension=0, tiled=True)  91.9 us
    reduce_scatter x1, waiting for transfers between devices, per_device(): lax.psum_scatter(jnp.dot(attended, w_out, preferred_element_type=jnp.floa...  85 us
    psum x1, waiting for transfers between devices, per_device(): lax.psum(grad_normed_two.astype(jnp.bfloat16), 'tensor').astype(jnp.float32)  79.8 us
    dot_general x5, matrix products, attend_back(): jnp.einsum('qhd,khd->hqk', grad_block, values, preferred_element_type=jnp...  75.3 us
  transfers between devices with their start and end apart: 15, of which 10 were waited for; matrix products, arithmetic and copies ran while one was open for 28% of the time, Pallas kernels for 0%

commit v1 on v0

--- a/solution.py
+++ b/solution.py
@@ -221,7 +221,9 @@
     expert_dot = jnp.sum(grad_all * expert_rows, axis=1)
     row_dots = jnp.stack([dense_dot, expert_dot], axis=1)
     grad_normed_two, row_dots = (
-        lax.psum(grad_normed_two.astype(jnp.bfloat16), "tensor").astype(jnp.float32),
+        jnp.sum(lax.all_gather(grad_normed_two.astype(jnp.bfloat16), "tensor"), axis=0).astype(
+            jnp.float32
+        ),
         lax.psum(row_dots.astype(jnp.bfloat16), "tensor").astype(jnp.float32),
     )
     mix_grad = jnp.stack([row_dots[:, 0], gate_prob * row_dots[:, 1]], axis=1)

time: 2370 us -> 2410 us (1.017)
  waiting for transfers between devices: 825 us -> 850 us
    all_gather x0 -> x1, waiting for transfers between devices: none -> 106 us  [per_device(): lax.all_gather(grad_normed_two.astype(jnp.bfloat16), 'tensor')]
    psum x1 -> x0, waiting for transfers between devices: 79.8 us -> none  [per_device(): lax.psum(grad_normed_two.astype(jnp.bfloat16), 'tensor').astype(jnp.float32)]
where the time goes in v1:
time: 2410 us
  waiting for transfers between devices  850 us (35%)
  matrix products  586 us (24%)
  blocking collectives  400 us (17%)
  other arithmetic  309 us (13%)
  local copies, waits for them, and re-layouts  217 us (9%)
    all_to_all x2, blocking collectives, to_owners(): lax.all_to_all(outgoing, 'expert', split_axis=0, concat_axis=0, tiled=True)  331 us
    all_to_all x2, waiting for transfers between devices, to_sources(): lax.all_to_all(parts.astype(jnp.bfloat16), 'expert', split_axis=0, concat...  267 us
    all_gather x1, waiting for transfers between devices, per_device(): lax.all_gather(grad_normed_two.astype(jnp.bfloat16), 'tensor')  106 us
    convert_element_type x5, other arithmetic, attend_back(): grad_scores = (weights * (grad_weights - inner)).astype(jnp.bfloat16)  101 us
    reduce_scatter x1, waiting for transfers between devices, per_device(): lax.psum_scatter(grad_down, 'expert', scatter_dimension=1, tiled=True)  92 us
    reduce_scatter x1, waiting for transfers between devices, per_device(): lax.psum_scatter(grad_up, 'expert', scatter_dimension=0, tiled=True)  91.8 us
    reduce_scatter x1, waiting for transfers between devices, per_device(): lax.psum_scatter(jnp.dot(attended, w_out, preferred_element_type=jnp.floa...  85 us
    dot_general x5, matrix products, attend_back(): jnp.einsum('qhd,khd->hqk', grad_block, values, preferred_element_type=jnp...  77.1 us
  transfers between devices with their start and end apart: 15, of which 10 were waited for; matrix products, arithmetic and copies ran while one was open for 28% of the time, Pallas kernels for 0%

profile of v1, /device:TPU:0, one launch (start us, length us, event | category | flops | bytes accessed | tf_op | source)
XLA Modules:
  0.0 2407.0 jit_solution(15231439711430115044)
XLA Ops:
  8.0 44.8 %all-gather.6.cloned.1.call-done = bf16[2560,1024]{1,0:T(8,128)(2,1)} async-done(((bf16[640,1024]{1,0:T(8,128)(2,1)}), bf16[2560,1024]{1,0:T(8,128)(2,1)}) %all-gather.6.cloned.1.call-update) | async-done | bytes 5242896 | tf_op jit(solution)/shard_map/all_gather | solution.py:121
  75.1 189.9 %while.33 = (s32[]{:T(128)}, bf16[5,512,256]{2,1,0:T(8,128)(2,1)}, f32[5,4,512]{2,1,0:T(4,128)S(1)}, s32[5]{0:T(128)S(1)}, s32[1,13]{1,0:T(1,128)S(1)}, /*index=...) while((s32[]{:T(128)}, bf16[5,512,256]{2,1,0:T(8,128)(2,1)}, ...), condition=%wide.region_7.8_spmd, body=%wide.region_2.7_spmd.sunk | while | flops 1414493696 | bytes 169976272 | solution.py:142
  272.6 85.0 %reduce-scatter.12.cloned.1.call-done = f32[640,1024]{1,0:T(8,128)} async-done(((f32[2560,1024]{1,0:T(8,128)}), f32[640,1024]{1,0:T(8,128)}) %reduce-scatter.12.cloned.1.call-update) | async-done | bytes 2621456 | tf_op jit(solution)/shard_map/reduce_scatter | solution.py:144
  368.6 63.2 %all-gather.8.cloned.1.call-done = f32[2560,1024]{1,0:T(8,128)} async-done(((f32[640,1024]{1,0:T(8,128)}), f32[2560,1024]{1,0:T(8,128)}) %all-gather.8.cloned.1.call-update) | async-done | bytes 10485776 | tf_op jit(solution)/shard_map/all_gather | solution.py:150
  441.6 18.1 scatter_custom_fusion
  459.7 166.5 %all_to_all.20 = bf16[8,4,112,1024]{3,2,1,0:T(8,128)(2,1)S(1)} all-to-all(bf16[8,4,112,1024]{3,2,1,0:T(8,128)(2,1)} %bitcast.212), channel_id=1, replica_groups=mesh['expert'=8,'tensor'=4] {'expert'}, dimensions={0} | all-to-all | bytes 14680064 | tf_op jit(solution)/shard_map/all_to_all | solution.py:88
  626.2 40.2 %fusion.43 = (bf16[3584,1024]{1,0:T(8,128)(2,1)S(1)}, f32[3584,1024]{1,0:T(8,128)}) fusion(bf16[3584,1024]{1,0:T(8,128)(2,1)S(1)} %bitcast.219, bf16[1,1024,1024]{2,1,0:T(8,128)(2,1)S(1)} %copy-done), kind=kOutput, calls=%fused_computation.106 | convolution fusion | flops 7754743808 | bytes 31457280 | tf_op jit(solution)/shard_map/dot_general | solution.py:171
  694.2 29.9 %fusion.62 = (bf16[2560,1024]{1,0:T(8,128)(2,1)}, f32[2560,1024]{1,0:T(8,128)}) fusion(bf16[2560,1024]{1,0:T(8,128)(2,1)S(1)} %multiply_convert_fusion.1, bf16[1024,1024]{1,0:T(8,128)(2,1)S(1)} %copy-done.64), kind=kOutput, calls=%fused_computation.135 | convolution fusion | flops 5539102720 | bytes 23068672 | tf_op jit(solution)/shard_map/dot_general | solution.py:153
  724.1 120.1 %all-to-all-done.1 = bf16[8,4,112,1024]{3,2,1,0:T(8,128)(2,1)} async-done(((bf16[8,4,112,1024]{3,2,1,0:T(8,128)(2,1)}), bf16[8,4,112,1024]{3,2,1,0:T(8,128)(2,1)}, u32[]{:S(2)}, u32[]{:S(2)}) %all-to-all-start.1) | async-done | bytes 7340064 | tf_op jit(solution)/shard_map/all_to_all | solution.py:92
  854.4 40.0 %gather_fusion = f32[2560,1024]{1,0:T(8,128)} fusion(f32[8,4,112,1024]{3,2,1,0:T(8,128)} %convert_element_type.173, s32[2560]{0:T(1024)S(1)} %copy-done.3), kind=kCustom, calls=%fused_computation | custom fusion | bytes 21002240 | tf_op jit(solution)/shard_map/gather | solution.py:178
  894.3 15.1 fusion.71
  920.1 17.7 scatter_custom_fusion.1
  937.7 164.2 %all_to_all.21 = bf16[8,4,112,1024]{3,2,1,0:T(8,128)(2,1)S(1)} all-to-all(bf16[8,4,112,1024]{3,2,1,0:T(8,128)(2,1)} %bitcast.213), channel_id=1, replica_groups=mesh['expert'=8,'tensor'=4] {'expert'}, dimensions={0} | all-to-all | bytes 14680064 | tf_op jit(solution)/shard_map/all_to_all | solution.py:88
  1101.9 15.5 fusion.49
  1148.4 146.4 %all-to-all-done.3 = bf16[8,4,112,1024]{3,2,1,0:T(8,128)(2,1)} async-done(((bf16[8,4,112,1024]{3,2,1,0:T(8,128)(2,1)}), bf16[8,4,112,1024]{3,2,1,0:T(8,128)(2,1)}, u32[]{:S(2)}, u32[]{:S(2)}) %all-to-all-start.3) | async-done | bytes 7340064 | tf_op jit(solution)/shard_map/all_to_all | solution.py:92
  1305.0 40.0 %gather_fusion.1 = f32[2560,1024]{1,0:T(8,128)} fusion(f32[8,4,112,1024]{3,2,1,0:T(8,128)} %convert_element_type.183, s32[2560]{0:T(1024)S(1)} %copy-done.3), kind=kCustom, calls=%fused_computation.1 | custom fusion | bytes 21002240 | tf_op jit(solution)/shard_map/gather | solution.py:220
  1381.3 105.6 %all-gather.12.cloned.1.call-done = bf16[10240,1024]{1,0:T(8,128)(2,1)} async-done(((bf16[2560,1024]{1,0:T(8,128)(2,1)}), bf16[10240,1024]{1,0:T(8,128)(2,1)}) %all-gather.12.cloned.1.call-update) | async-done | bytes 20971536 | tf_op jit(solution)/shard_map/all_gather | solution.py:224
  1526.0 420.9 %while.34 = (s32[]{:T(128)}, f32[2560,256]{0,1:T(8,128)}, f32[2560,256]{0,1:T(8,128)}, bf16[5,512,256]{2,1,0:T(8,128)(2,1)}, bf16[3,2560,256]{1,2,0:T(8,128)(2,1...) while((s32[]{:T(128)}, f32[2560,256]{0,1:T(8,128)}, ...), condition=%wide.region_33.34_spmd.clone, body=%wide.region_29.33_spmd.clone.sunk | while | flops 3446896640 | bytes 251757168 | solution.py:290
  1556.4 16.8 multiply_reduce_fusion.11
  1573.2 20.6 multiply_convert_fusion.9
  1642.3 15.1 multiply_reduce_fusion.11
  1657.3 20.0 multiply_convert_fusion.9
  1725.9 15.1 multiply_reduce_fusion.11
  1740.9 20.0 multiply_convert_fusion.9
  1824.5 20.0 multiply_convert_fusion.9
  1908.1 20.0 multiply_convert_fusion.9
  2035.6 21.6 all-reduce
  2069.5 37.1 %psum.15 = f32[1024]{0:T(1024)} all-reduce(f32[1024]{0:T(1024)S(1)} %get-tuple-element.473), channel_id=1, replica_groups=mesh['expert'=8,'tensor'=4] {'expert','tensor'}, use_global_device_ids=true, to_apply=%region_38.39 | all-reduce | flops 1024 | bytes 8192 | tf_op jit(solution)/shard_map/psum | solution.py:323
  2116.4 32.1 %reduce-scatter.26.cloned.1.call-done = f32[128,8]{0,1:T(8,128)} async-done(((f32[1024,8]{0,1:T(8,128)}), f32[128,8]{0,1:T(8,128)}) %reduce-scatter.26.cloned.1.call-update) | async-done | bytes 4112 | tf_op jit(solution)/shard_map/reduce_scatter | solution.py:320
  2148.5 92.0 %reduce-scatter.24.cloned.1.call-done = f32[1024,128]{1,0:T(8,128)} async-done(((f32[1024,1024]{1,0:T(8,128)}), f32[1024,128]{1,0:T(8,128)}) %reduce-scatter.24.cloned.1.call-update) | async-done | bytes 524304 | tf_op jit(solution)/shard_map/reduce_scatter | solution.py:319
  2240.5 91.8 %reduce-scatter.22.cloned.1.call-done = f32[128,1024]{1,0:T(8,128)} async-done(((f32[1024,1024]{1,0:T(8,128)}), f32[128,1024]{1,0:T(8,128)}) %reduce-scatter.22.cloned.1.call-update) | async-done | bytes 524304 | tf_op jit(solution)/shard_map/reduce_scatter | solution.py:318
  2332.3 68.0 %reduce-scatter.20.cloned.1.call-done = f32[256,128]{1,0:T(8,128)} async-done(((f32[256,1024]{1,0:T(8,128)}), f32[256,128]{1,0:T(8,128)}) %reduce-scatter.20.cloned.1.call-update) | async-done | bytes 131088 | tf_op jit(solution)/shard_map/reduce_scatter | solution.py:316
  (495 shorter events, 770.8 us)
Async XLA Ops:
  7.2 619.0 %copy-start = (bf16[1,1024,1024]{2,1,0:T(8,128)(2,1)S(1)}, bf16[1,1024,1024]{2,1,0:T(8,128)(2,1)}, u32[]{:S(2)}) copy-start(bf16[1,1024,1024]{2,1,0:T(8,128)(2,1)} %param.30) | copy-start | bytes 6291460
  7.2 45.6 %all-gather.6.cloned.1.call-start = ((), (), s32[]{:S(2)}) async-start(), calls=%async_computation.13 | async-start | bytes 6553600 | tf_op jit(solution)/shard_map/all_gather | solution.py:121
  7.9 349.6 %reduce-scatter.12.cloned.1.call-start = ((), (), s32[]{:S(2)}) async-start(), calls=%async_computation.14 | async-start | bytes 13107200 | tf_op jit(solution)/shard_map/reduce_scatter | solution.py:144
  265.0 92.6 %copy-start.16 = (bf16[640,1024]{1,0:T(8,128)(2,1)S(1)}, bf16[640,1024]{1,0:T(8,128)(2,1)}, u32[]{:S(2)}) copy-start(bf16[640,1024]{1,0:T(8,128)(2,1)} %param.18) | copy-start | bytes 3932164
  272.1 96.3 %copy-start.60 = (s32[3]{0:T(128)S(1)}, s32[3]{0:T(128)}, u32[]{:S(2)}) copy-start(s32[3]{0:T(128)} %constant.393) | copy-start | bytes 40
  272.1 96.4 %copy-start.59 = (s32[3]{0:T(128)S(1)}, s32[3]{0:T(128)}, u32[]{:S(2)}) copy-start(s32[3]{0:T(128)} %constant.396) | copy-start | bytes 40
  272.1 159.7 %all-gather.8.cloned.1.call-start = ((), (), s32[]{:S(2)}) async-start(), calls=%async_computation.15 | async-start | bytes 13107200 | tf_op jit(solution)/shard_map/all_gather | solution.py:150
  361.5 332.0 %copy-start.27 = (s32[2560]{0:T(1024)}, s32[2560]{0:T(1024)S(1)}, u32[]{:S(2)}) copy-start(s32[2560]{0:T(1024)S(1)} %reduce.9) | copy-start | bytes 30724
  436.3 248.6 %copy-start.23 = (f32[2560]{0:T(1024)}, f32[2560]{0:T(1024)S(1)}, u32[]{:S(2)}) copy-start(f32[2560]{0:T(1024)S(1)} %broadcast_multiply_fusion.2) | copy-start | bytes 30724
  441.6 243.4 %copy-start.25 = (f32[2560]{0:T(1024)}, f32[2560]{0:T(1024)S(1)}, u32[]{:S(2)}) copy-start(f32[2560]{0:T(1024)S(1)} %add_rsqrt_fusion) | copy-start | bytes 30724
  679.4 164.8 %all-to-all-start.1 = ((bf16[8,4,112,1024]{3,2,1,0:T(8,128)(2,1)}), bf16[8,4,112,1024]{3,2,1,0:T(8,128)(2,1)}, u32[]{:S(2)}, u32[]{:S(2)}) async-start(bf16[8,4,112,1024]{3,2,1,0:T(8,128)(2,1)} %convolution_convert_fusion.1), calls=%async_computation.2 | async-start | bytes 14680064 | tf_op jit(solution)/shard_map/all_to_all | solution.py:92
  684.3 210.0 %all-gather.10.cloned.1.call-start = ((), (), s32[]{:S(2)}) async-start(), calls=%async_computation.17 | async-start | bytes 6553600 | tf_op jit(solution)/shard_map/all_gather | solution.py:193
  724.1 130.3 %copy-start.3 = (s32[2560]{0:T(1024)S(1)}, s32[2560]{0:T(1024)}, u32[]{:S(2)}) copy-start(s32[2560]{0:T(1024)} %get-tuple-element.475) | copy-start | bytes 30724
  919.8 436.8 %copy-start.39 = (f32[2560,1]{0,1:T(1,128)}, f32[2560,1]{0,1:T(1,128)S(1)}, u32[]{:S(2)}) copy-start(f32[2560,1]{0,1:T(1,128)S(1)} %reshape_multiply_fusion) | copy-start | bytes 30724
  919.9 436.7 %copy-start.33 = (f32[2560,2]{0,1:T(2,128)}, f32[2560,2]{0,1:T(2,128)S(1)}, u32[]{:S(2)}) copy-start(f32[2560,2]{0,1:T(2,128)S(1)} %get-tuple-element.458) | copy-start | bytes 61444
  919.9 436.7 %copy-start.47 = (f32[2560]{0:T(1024)}, f32[2560]{0:T(1024)S(1)}, u32[]{:S(2)}) copy-start(f32[2560]{0:T(1024)S(1)} %get-tuple-element.457) | copy-start | bytes 30724
  920.0 441.5 %copy-start.49 = (f32[2560]{0:T(1024)}, f32[2560]{0:T(1024)S(1)}, u32[]{:S(2)}) copy-start(f32[2560]{0:T(1024)S(1)} %get-tuple-element.426) | copy-start | bytes 30724
  937.7 164.2 %copy-start.62 = (bf16[1,1024,1024]{2,1,0:T(8,128)(2,1)S(1)}, bf16[1,1024,1024]{2,1,0:T(8,128)(2,1)}, u32[]{:S(2)}) copy-start(bf16[1,1024,1024]{2,1,0:T(8,128)(2,1)} %param.31) | copy-start | bytes 6291460
  1130.4 164.4 %all-to-all-start.3 = ((bf16[8,4,112,1024]{3,2,1,0:T(8,128)(2,1)}), bf16[8,4,112,1024]{3,2,1,0:T(8,128)(2,1)}, u32[]{:S(2)}, u32[]{:S(2)}) async-start(bf16[8,4,112,1024]{3,2,1,0:T(8,128)(2,1)} %convolution_convert_fusion), calls=%async_computation.5 | async-start | bytes 14680064 | tf_op jit(solution)/shard_map/all_to_all | solution.py:92
  1135.4 351.5 %all-gather.12.cloned.1.call-start = ((), (), s32[]{:S(2)}) async-start(), calls=%async_computation.24 | async-start | bytes 26214400 | tf_op jit(solution)/shard_map/all_gather | solution.py:224
  1356.5 643.7 %reduce-scatter.28.cloned.1.call-start = ((), (), s32[]{:S(2)}) async-start(), calls=%async_computation.25 | async-start | bytes 589824
  1375.5 626.1 %reduce-scatter.14.cloned.1.call-start = ((), (), s32[]{:S(2)}) async-start(), calls=%async_computation.16 | async-start | bytes 6553600 | tf_op jit(solution)/shard_map/reduce_scatter | solution.py:182
  1381.2 725.4 %reduce-scatter.18.cloned.1.call-start = ((), (), s32[]{:S(2)}) async-start(), calls=%async_computation.19 | async-start | bytes 3538944 | tf_op jit(solution)/shard_map/reduce_scatter | solution.py:315
  1526.0 425.7 %copy-start.36 = (f32[2560]{0:T(1024)S(1)}, f32[2560]{0:T(1024)}, u32[]{:S(2)}) copy-start(f32[2560]{0:T(1024)} %copy-done.35) | copy-start | bytes 30724
  1526.0 425.7 %copy-start.42 = (f32[2560]{0:T(1024)S(1)}, f32[2560]{0:T(1024)}, u32[]{:S(2)}) copy-start(f32[2560]{0:T(1024)} %copy-done.41) | copy-start | bytes 30724
  1526.0 425.7 %copy-start.56 = (f32[1024]{0:T(1024)S(1)}, f32[1024]{0:T(1024)}, u32[]{:S(2)}) copy-start(f32[1024]{0:T(1024)} %param.22) | copy-start | bytes 12292
  1961.4 147.1 %reduce-scatter.16.cloned.1.call-start = ((), (), s32[]{:S(2)}) async-start(), calls=%async_computation.18 | async-start | bytes 6553600 | tf_op jit(solution)/shard_map/reduce_scatter | solution.py:307
  1973.4 175.1 %reduce-scatter.26.cloned.1.call-start = ((), (), s32[]{:S(2)}) async-start(), calls=%async_computation.23 | async-start | bytes 36864 | tf_op jit(solution)/shard_map/reduce_scatter | solution.py:320
  1977.4 263.1 %reduce-scatter.24.cloned.1.call-start = ((), (), s32[]{:S(2)}) async-start(), calls=%async_computation.22 | async-start | bytes 4718592 | tf_op jit(solution)/shard_map/reduce_scatter | solution.py:319
  1988.1 344.2 %reduce-scatter.22.cloned.1.call-start = ((), (), s32[]{:S(2)}) async-start(), calls=%async_computation.21 | async-start | bytes 4718592 | tf_op jit(solution)/shard_map/reduce_scatter | solution.py:318
  1998.8 401.5 %reduce-scatter.20.cloned.1.call-start = ((), (), s32[]{:S(2)}) async-start(), calls=%async_computation.20 | async-start | bytes 1179648 | tf_op jit(solution)/shard_map/reduce_scatter | solution.py:316
  2057.8 342.4 %copy-start.1 = (bf16[1,1024,1024]{2,1,0:T(8,128)(2,1)S(1)}, bf16[1,1024,1024]{2,1,0:T(8,128)(2,1)}, u32[]{:S(2)}) copy-start(bf16[1,1024,1024]{2,1,0:T(8,128)(2,1)} %param.30) | copy-start | bytes 6291460
  (86 other events, 1126.2 us)
Sparse Core Ops, SparseCore 0:
  9.6 43.1 all-gather.5
  272.2 85.2 reduce-scatter.11
  361.6 70.1 all-gather.7
  686.4 40.8 all-gather.9
  1356.7 130.1 all-gather.11
  1490.1 61.8 reduce-scatter.27
  1554.7 50.5 reduce-scatter.13
  1961.5 75.7 reduce-scatter.17
  2039.9 51.2 reduce-scatter.15
  2095.0 53.4 reduce-scatter.25
  2153.1 87.3 reduce-scatter.23
  2244.6 87.6 reduce-scatter.21
  2336.6 63.5 reduce-scatter.19
